TPU v7x, 32 devices: a whole 2x2x4 slice. The times are simulated.
32 devices in a mesh: row: 8 (over z, x), col: 4 (over y, core).
Axes of the slice: x: 2, y: 2, z: 4, core: 2. Of those that a mesh axis runs over, the one named last changes fastest.
Arguments:
- tokens: bfloat16 [512, 8192], P('col', 'row'), may hold values from -6 to 6
- gate_weight: bfloat16 [8192, 14336], P('row', 'col'), may hold values from -0.09375 to 0.09375
- up_weight: bfloat16 [8192, 14336], P('row', 'col'), may hold values from -0.09375 to 0.09375
- down_weight: bfloat16 [14336, 8192], P('col', 'row'), may hold values from -0.09375 to 0.09375
- gate_mask: int32 [128, 224], P('row', 'col'), may hold values from 0 to 1, as said below
- up_mask: int32 [128, 224], P('row', 'col'), may hold values from 0 to 1, as said below
- down_mask: int32 [224, 128], P('col', 'row'), may hold values from 0 to 1, as said below
- head_weight: bfloat16 [8192, 128], P('row'), may hold values from -0.15625 to 0.15625
- labels: int32 [512], P('col'), may hold values from 0 to 127
Outputs:
- token_loss: float32 [512], P('col')
- tokens_grad: bfloat16 [512, 8192], P('col', 'row')
- gate_grad: bfloat16 [8192, 14336], P('row', 'col')
- up_grad: bfloat16 [8192, 14336], P('row', 'col')
- down_grad: bfloat16 [14336, 8192], P('col', 'row')
Inputs may be any that keep to these rules, and one draw needn't show every extreme that they name: `gate_mask`: 1 keeps a block of 64 x 64 weights, 0 prunes it. `up_mask`: 1 keeps a block of 64 x 64 weights, 0 prunes it. `down_mask`: 1 keeps a block of 64 x 64 weights, 0 prunes it.
All inputs are finite; a program needn't handle non-finite values.
Results may differ from a plain program's by a relative error of at most 0.011.
Values may be sent and summed in bfloat16 or wider, within the bound.
A program may use at most 192 MiB of HBM per device.

v0:
```python
import jax
import jax.numpy as jnp
from jax import lax
from jax.sharding import PartitionSpec as P

loss_scale = 8.0


def masked(weight, block_mask):
    height, breadth = weight.shape
    blocks = weight.reshape(
        block_mask.shape[0],
        height // block_mask.shape[0],
        block_mask.shape[1],
        breadth // block_mask.shape[1],
    )
    pruned = blocks * block_mask[:, None, :, None].astype(weight.dtype)
    return pruned.reshape(height, breadth)


def classify(logits, labels):
    exponent = jnp.exp(logits)
    partition = jnp.sum(exponent, axis=1, keepdims=True)
    classes = lax.broadcasted_iota(jnp.int32, logits.shape, 1)
    onehot = (labels[:, None] == classes).astype(jnp.float32)
    token_cost = jnp.log(partition[:, 0]) - jnp.sum(logits * onehot, axis=1)
    return (token_cost, loss_scale * (exponent / partition - onehot))


def token_product(panel_rows, weight, weight_axis):
    panel_axis = 0
    return lax.dot_general(
        panel_rows,
        weight,
        (((panel_axis,), (weight_axis,)), ((), ())),
        preferred_element_type=jnp.float32,
    )


def shards(
    tokens, gate_weight, up_weight, down_weight, gate_mask, up_mask, down_mask, head_weight, labels
):
    gate_kept = masked(gate_weight, gate_mask)
    up_kept = masked(up_weight, up_mask)
    down_kept = masked(down_weight, down_mask)
    every_token = lax.all_gather(tokens, "col", axis=0, tiled=True)
    gate_part = lax.dot_general(
        gate_kept, every_token, (((0,), (1,)), ((), ())), preferred_element_type=jnp.float32
    )
    up_part = lax.dot_general(
        up_kept, every_token, (((0,), (1,)), ((), ())), preferred_element_type=jnp.float32
    )
    stacked = lax.psum_scatter(
        jnp.concatenate([gate_part, up_part], axis=1), "row", scatter_dimension=0, tiled=True
    )
    midpoint = stacked.shape[1] // 2
    gate_sum = stacked[:, :midpoint]
    up_sum = stacked[:, midpoint:]
    sigmoid_gate = jax.nn.sigmoid(gate_sum)
    activated = gate_sum * sigmoid_gate
    hidden = (activated * up_sum).astype(jnp.bfloat16)
    hidden_all = lax.all_gather(hidden, "row", axis=0, tiled=True)
    branch = lax.psum_scatter(
        token_product(hidden_all, down_kept, 0), "col", scatter_dimension=0, tiled=True
    )
    mixed_rows = (tokens.astype(jnp.float32) + branch).astype(jnp.bfloat16)
    partial_value = jnp.dot(mixed_rows, head_weight, preferred_element_type=jnp.float32)
    logits = lax.psum(partial_value, "row")
    token_loss, grad_full = classify(logits, labels)
    dlogits = grad_full.astype(jnp.bfloat16)
    dmixed = lax.dot_general(
        dlogits, head_weight, (((1,), (1,)), ((), ())), preferred_element_type=jnp.float32
    ).astype(jnp.bfloat16)
    dmixed_all = lax.all_gather(dmixed, "col", axis=0, tiled=True)
    dhidden = lax.psum_scatter(
        lax.dot_general(
            down_kept, dmixed_all, (((1,), (1,)), ((), ())), preferred_element_type=jnp.float32
        ),
        "row",
        scatter_dimension=0,
        tiled=True,
    )
    gate_delta = (dhidden * up_sum * sigmoid_gate * (1.0 + gate_sum * (1.0 - sigmoid_gate))).astype(
        jnp.bfloat16
    )
    up_delta = (dhidden * activated).astype(jnp.bfloat16)
    gate_all, up_all = (
        lax.all_gather(gate_delta, "row", axis=0, tiled=True),
        lax.all_gather(up_delta, "row", axis=0, tiled=True),
    )
    token_axis = 1
    down_grad = masked(
        lax.dot_general(
            hidden_all,
            dmixed_all,
            (((token_axis,), (0,)), ((), ())),
            preferred_element_type=jnp.float32,
        ),
        down_mask,
    ).astype(jnp.bfloat16)
    gate_grad = masked(
        lax.dot_general(
            every_token,
            gate_all,
            (((0,), (token_axis,)), ((), ())),
            preferred_element_type=jnp.float32,
        ),
        gate_mask,
    ).astype(jnp.bfloat16)
    up_grad = masked(
        lax.dot_general(
            every_token,
            up_all,
            (((0,), (token_axis,)), ((), ())),
            preferred_element_type=jnp.float32,
        ),
        up_mask,
    ).astype(jnp.bfloat16)
    gate_term = token_product(gate_all, gate_kept, 1)
    up_term = token_product(up_all, up_kept, 1)
    input_sum = lax.psum_scatter(gate_term + up_term, "col", scatter_dimension=0, tiled=True)
    tokens_grad = (dmixed.astype(jnp.float32) + input_sum).astype(jnp.bfloat16)
    return (token_loss, tokens_grad, gate_grad, up_grad, down_grad)


def solution(mesh):
    placed = (
        P("col", "row"),
        P("row", "col"),
        P("row", "col"),
        P("col", "row"),
        P("row", "col"),
        P("row", "col"),
        P("col", "row"),
        P("row", None),
        P("col"),
    )
    return jax.shard_map(
        shards,
        mesh=mesh,
        in_specs=placed,
        out_specs=(P("col"), P("col", "row"), P("row", "col"), P("row", "col"), P("col", "row")),
        check_vma=False,
    )
```

profile of v0, /device:TPU:0, one launch (start us, length us, event | category | flops | bytes accessed | tf_op | source)
XLA Modules:
  0.0 1011.9 jit_solution(17688586089172399964)
XLA Ops:
  15.9 18.9 %mul.100 = bf16[1024,3584]{1,0:T(8,128)(2,1)} reshape(bf16[16,64,56,64]{3,2,1,0:T(8,128)(2,1)} %mul.99) | data formatting | bytes 14680064 | tf_op jit(solution)/shard_map/mul | solution.py:17
  34.9 7.2 mul.96
  42.0 18.7 %mul.97 = bf16[1024,3584]{1,0:T(8,128)(2,1)} reshape(bf16[16,64,56,64]{3,2,1,0:T(8,128)(2,1)} %mul.96) | data formatting | bytes 14680064 | tf_op jit(solution)/shard_map/mul | solution.py:17
  60.8 10.2 %mul.101 = bf16[1024,3584]{1,0:T(8,128)(2,1)} multiply(bf16[1024,3584]{1,0:T(8,128)(2,1)} %param.11, bf16[1024,3584]{1,0:T(8,128)(2,1)} %mul.100) | non-fusion elementwise | flops 3670016 | bytes 22020096 | tf_op jit(solution)/shard_map/mul | solution.py:17
  71.0 10.2 %mul.98 = bf16[1024,3584]{1,0:T(8,128)(2,1)} multiply(bf16[1024,3584]{1,0:T(8,128)(2,1)} %param.10, bf16[1024,3584]{1,0:T(8,128)(2,1)} %mul.97) | non-fusion elementwise | flops 3670016 | bytes 22020096 | tf_op jit(solution)/shard_map/mul | solution.py:17
  97.3 15.7 %copy.43 = f32[3584,1024]{1,0:T(8,128)} copy(f32[3584,1024]{0,1:T(8,128)} %pad_maximum_fusion) | data formatting | bytes 29360128
  113.1 239.5 %reduce-scatter.13.cloned.1.call-done = f32[448,1024]{1,0:T(8,128)} async-done(((f32[3584,1024]{1,0:T(8,128)}), f32[448,1024]{1,0:T(8,128)}) %reduce-scatter.13.cloned.1.call-update) | async-done | bytes 1835024 | tf_op jit(solution)/shard_map/reduce_scatter | solution.py:53
  355.3 7.2 mul.104
  362.5 20.1 %mul.105 = bf16[3584,1024]{1,0:T(8,128)(2,1)} reshape(bf16[56,64,16,64]{3,2,1,0:T(8,128)(2,1)} %mul.104) | data formatting | bytes 14680064 | tf_op jit(solution)/shard_map/mul | solution.py:17
  382.6 12.5 %mul.106 = bf16[3584,1024]{1,0:T(8,128)(2,1)} multiply(bf16[3584,1024]{1,0:T(8,128)(2,1)} %param.12, bf16[3584,1024]{1,0:T(8,128)(2,1)} %mul.105) | non-fusion elementwise | flops 3670016 | bytes 22020096 | tf_op jit(solution)/shard_map/mul | solution.py:17
  395.1 25.5 %all-gather.8.cloned.1.call-done = bf16[3584,512]{1,0:T(8,128)(2,1)} async-done(((bf16[448,512]{1,0:T(8,128)(2,1)}), bf16[3584,512]{1,0:T(8,128)(2,1)}) %all-gather.8.cloned.1.call-update) | async-done | bytes 3670032 | tf_op jit(solution)/shard_map/all_gather | solution.py:62
  420.6 9.5 fusion.11
  430.2 30.0 %reduce-scatter.9.cloned.1.call-done = f32[128,1024]{1,0:T(8,128)} async-done(((f32[512,1024]{1,0:T(8,128)}), f32[128,1024]{1,0:T(8,128)}) %reduce-scatter.9.cloned.1.call-update) | async-done | bytes 524304 | tf_op jit(solution)/shard_map/reduce_scatter | solution.py:63
  462.1 71.2 %all-reduce.2.cloned.1.call-done = f32[128,128]{1,0:T(8,128)} async-done(((f32[128,128]{1,0:T(8,128)}), f32[128,128]{1,0:T(8,128)}) %all-reduce.2.cloned.1.call-update) | async-done | bytes 65552 | tf_op jit(solution)/shard_map/psum | solution.py:68
  536.4 16.6 %all-gather.10.cloned.1.call-done = bf16[512,1024]{1,0:T(8,128)(2,1)} async-done(((bf16[128,1024]{1,0:T(8,128)(2,1)}), bf16[512,1024]{1,0:T(8,128)(2,1)}) %all-gather.10.cloned.1.call-update) | async-done | bytes 1048592 | tf_op jit(solution)/shard_map/all_gather | solution.py:74
  553.0 10.3 %fusion.12 = f32[3584,512]{1,0:T(8,128)} fusion(bf16[3584,1024]{1,0:T(8,128)(2,1)} %mul.106, bf16[512,1024]{1,0:T(8,128)(2,1)} %all-gather.10.cloned.1.call-done), kind=kOutput, calls=%fused_computation.29 | convolution fusion | flops 3758096384 | bytes 15728640
  563.3 133.0 %reduce-scatter.15.cloned.1.call-done = f32[448,512]{1,0:T(8,128)} async-done(((f32[3584,512]{1,0:T(8,128)}), f32[448,512]{1,0:T(8,128)}) %reduce-scatter.15.cloned.1.call-update) | async-done | bytes 917520 | tf_op jit(solution)/shard_map/reduce_scatter | solution.py:75
  699.7 64.6 %all-gather.12.cloned.1.call-done = bf16[3584,512]{1,0:T(8,128)(2,1)} async-done(((bf16[448,512]{1,0:T(8,128)(2,1)}), bf16[3584,512]{1,0:T(8,128)(2,1)}) %all-gather.12.cloned.1.call-update) | async-done | bytes 3670032 | tf_op jit(solution)/shard_map/all_gather | solution.py:88
  764.4 9.5 fusion.13
  773.9 57.6 %all-gather.14.cloned.1.call-done = bf16[3584,512]{1,0:T(8,128)(2,1)} async-done(((bf16[448,512]{1,0:T(8,128)(2,1)}), bf16[3584,512]{1,0:T(8,128)(2,1)}) %all-gather.14.cloned.1.call-update) | async-done | bytes 3670032 | tf_op jit(solution)/shard_map/all_gather | solution.py:89
  831.5 10.1 convolution_add_fusion
  841.9 12.7 %mul.115 = f32[16,64,56,64]{1,0,3,2:T(8,128)} broadcast(f32[16,56]{0,1:T(8,128)S(1)} %copy.37), dimensions={0,2} | broadcast | bytes 14683648 | tf_op jit(solution)/shard_map/mul | solution.py:17
  854.6 25.2 %mul.116 = f32[1024,3584]{0,1:T(8,128)} reshape(f32[16,64,56,64]{1,0,3,2:T(8,128)} %mul.115) | data formatting | bytes 29360128 | tf_op jit(solution)/shard_map/mul | solution.py:17
  879.8 11.6 %mul.118 = f32[16,64,56,64]{1,0,3,2:T(8,128)} broadcast(f32[16,56]{0,1:T(8,128)S(1)} %copy.38), dimensions={0,2} | broadcast | bytes 14683648 | tf_op jit(solution)/shard_map/mul | solution.py:17
  891.4 24.9 %mul.119 = f32[1024,3584]{0,1:T(8,128)} reshape(f32[16,64,56,64]{1,0,3,2:T(8,128)} %mul.118) | data formatting | bytes 29360128 | tf_op jit(solution)/shard_map/mul | solution.py:17
  916.3 11.6 %mul.121 = f32[56,64,16,64]{3,2,1,0:T(8,128)} broadcast(f32[56,16]{1,0:T(8,128)S(1)} %copy.39), dimensions={0,2} | broadcast | bytes 14683648 | tf_op jit(solution)/shard_map/mul | solution.py:17
  928.0 25.0 %mul.122 = f32[3584,1024]{1,0:T(8,128)} reshape(f32[56,64,16,64]{3,2,1,0:T(8,128)} %mul.121) | data formatting | bytes 29360128 | tf_op jit(solution)/shard_map/mul | solution.py:17
  953.5 10.3 %multiply_convert_fusion = bf16[3584,1024]{1,0:T(8,128)(2,1)} fusion(f32[3584,1024]{1,0:T(8,128)} %mul.122, bf16[3584,512]{1,0:T(8,128)(2,1)} %all-gather.8.cloned.1.call-done, bf16[512,1024]{1,0:T(8,128)(2,1)S(1)} %copy-done.8), kind=kOutput, calls=%fused_computation.5 | convolution fusion | flops 3765436416 | bytes 26738688 | tf_op jit(solution)/shard_map/dot_general | solution.py:93
  963.8 9.1 fusion.1
  972.9 9.9 copy.40
  982.8 10.2 %fusion = bf16[1024,3584]{0,1:T(8,128)(2,1)} fusion(f32[1024,3584]{0,1:T(8,128)} %mul.119, bf16[3584,512]{1,0:T(8,128)(2,1)} %all-gather.14.cloned.1.call-done, bf16[512,1024]{1,0:T(8,128)(2,1)S(1)} %copy-done.5), kind=kOutput, calls=%fused_computation.2 | convolution fusion | flops 3765436416 | bytes 26738688 | tf_op jit(solution)/shard_map/dot_general | solution.py:111
  993.0 10.0 copy.41
  (64 shorter events, 38.7 us)
Async XLA Ops:
  7.2 453.0 %copy-start = (bf16[1024,128]{1,0:T(8,128)(2,1)S(1)}, bf16[1024,128]{1,0:T(8,128)(2,1)}, u32[]{:S(2)}) copy-start(bf16[1024,128]{1,0:T(8,128)(2,1)} %param.16) | copy-start | bytes 786436
  7.2 74.0 %all-gather.6.cloned.1.call-start = ((), (), s32[]{:S(2)}) async-start(), calls=%async_computation.4 | async-start | bytes 1310720 | tf_op jit(solution)/shard_map/all_gather | solution.py:46
  7.9 344.7 %reduce-scatter.13.cloned.1.call-start = ((), (), s32[]{:S(2)}) async-start(), calls=%async_computation.12 | async-start | bytes 16515072 | tf_op jit(solution)/shard_map/reduce_scatter | solution.py:53
  15.9 18.9 %copy-start.9 = (s32[16,56]{1,0:T(8,128)S(1)}, s32[16,56]{1,0:T(8,128)}, u32[]{:S(2)}) copy-start(s32[16,56]{1,0:T(8,128)} %param.13) | copy-start | bytes 10756
  81.2 6.7 copy-start.4
  81.2 6.7 copy-start.5
  113.0 242.2 %copy-start.10 = (s32[56,16]{0,1:T(8,128)S(1)}, s32[56,16]{0,1:T(8,128)}, u32[]{:S(2)}) copy-start(s32[56,16]{0,1:T(8,128)} %param.15) | copy-start | bytes 10756
  113.0 307.6 %all-gather.8.cloned.1.call-start = ((), (), s32[]{:S(2)}) async-start(), calls=%async_computation.5 | async-start | bytes 4128768 | tf_op jit(solution)/shard_map/all_gather | solution.py:62
  355.1 105.0 %reduce-scatter.9.cloned.1.call-start = ((), (), s32[]{:S(2)}) async-start(), calls=%async_computation.6 | async-start | bytes 2621440 | tf_op jit(solution)/shard_map/reduce_scatter | solution.py:63
  395.1 65.1 %copy-start.7 = (bf16[128,1024]{1,0:T(8,128)(2,1)S(1)}, bf16[128,1024]{1,0:T(8,128)(2,1)}, u32[]{:S(2)}) copy-start(bf16[128,1024]{1,0:T(8,128)(2,1)} %param.9) | copy-start | bytes 786436
  395.1 138.2 %copy-start.11 = (s32[128]{0:T(128)S(1)}, s32[128]{0:T(128)}, u32[]{:S(2)}) copy-start(s32[128]{0:T(128)} %param.17) | copy-start | bytes 1540
  430.1 103.2 %all-reduce.2.cloned.1.call-start = ((), (), s32[]{:S(2)}) async-start(), calls=%async_computation.7 | async-start | bytes 131072 | tf_op jit(solution)/shard_map/psum | solution.py:68
  462.1 90.9 %all-gather.10.cloned.1.call-start = ((), (), s32[]{:S(2)}) async-start(), calls=%async_computation.8 | async-start | bytes 1310720 | tf_op jit(solution)/shard_map/all_gather | solution.py:74
  536.2 160.1 %reduce-scatter.15.cloned.1.call-start = ((), (), s32[]{:S(2)}) async-start(), calls=%async_computation.13 | async-start | bytes 8257536 | tf_op jit(solution)/shard_map/reduce_scatter | solution.py:75
  563.2 133.1 %copy-start.3 = (f32[448,1024]{1,0:T(8,128)S(1)}, f32[448,1024]{1,0:T(8,128)}, u32[]{:S(2)}) copy-start(f32[448,1024]{1,0:T(8,128)} %reduce-scatter.13.cloned.1.call-done) | copy-start | bytes 5505028
  563.3 201.1 %all-gather.12.cloned.1.call-start = ((), (), s32[]{:S(2)}) async-start(), calls=%async_computation.9 | async-start | bytes 4128768 | tf_op jit(solution)/shard_map/all_gather | solution.py:88
  699.0 132.6 %all-gather.14.cloned.1.call-start = ((), (), s32[]{:S(2)}) async-start(), calls=%async_computation.10 | async-start | bytes 4128768 | tf_op jit(solution)/shard_map/all_gather | solution.py:89
  699.7 303.3 %reduce-scatter.11.cloned.1.call-start = ((), (), s32[]{:S(2)}) async-start(), calls=%async_computation.11 | async-start | bytes 2621440 | tf_op jit(solution)/shard_map/reduce_scatter | solution.py:121
  928.0 25.5 %copy-start.8 = (bf16[512,1024]{1,0:T(8,128)(2,1)S(1)}, bf16[512,1024]{1,0:T(8,128)(2,1)}, u32[]{:S(2)}) copy-start(bf16[512,1024]{1,0:T(8,128)(2,1)} %all-gather.10.cloned.1.call-done) | copy-start | bytes 3145732
  953.5 10.3 %copy-start.2 = (bf16[3584,512]{1,0:T(8,128)(2,1)S(1)}, bf16[3584,512]{1,0:T(8,128)(2,1)}, u32[]{:S(2)}) copy-start(bf16[3584,512]{1,0:T(8,128)(2,1)} %all-gather.12.cloned.1.call-done) | copy-start | bytes 11010052
  982.8 22.0 %copy-start.1 = (bf16[1024,128]{1,0:T(8,128)(2,1)S(1)}, bf16[1024,128]{1,0:T(8,128)(2,1)}, u32[]{:S(2)}) copy-start(bf16[1024,128]{1,0:T(8,128)(2,1)} %param.16) | copy-start | bytes 786436
  993.0 10.0 copy-start.6
Sparse Core Ops, SparseCore 0:
  9.5 19.4 all-gather.5
  113.2 239.4 reduce-scatter.12
  355.3 65.2 all-gather.7
  430.2 29.8 reduce-scatter.8
  464.0 69.2 all-reduce.1
  536.3 16.6 all-gather.9
  563.4 132.8 reduce-scatter.14
  699.1 65.2 all-gather.11
  766.6 64.9 all-gather.13
  841.8 29.8 reduce-scatter.10
where the time goes:
time: 1020 us; the launch traced here: 1010 us
  waiting for transfers between devices  640 us (63%)
  local copies, waits for them, and re-layouts  226 us (22%)
  matrix products  83.3 us (8%)
  other arithmetic  47.7 us (5%)
  between operations  14.5 us (1%)
    reduce_scatter x1, waiting for transfers between devices, shards(): lax.psum_scatter(jnp.concatenate([gate_part, up_part], axis=1), 'row', sc...  240 us
    mul x12, local copies, waits for them, and re-layouts, masked(): pruned = blocks * block_mask[:, None, :, None].astype(weight.dtype)  190 us
    reduce_scatter x1, waiting for transfers between devices, shards(): lax.psum_scatter(lax.dot_general(down_kept, dmixed_all, (((1,), (1,)), ((...  133 us
    psum x1, waiting for transfers between devices, shards(): logits = lax.psum(partial_value, 'row')  71.2 us
    all_gather x1, waiting for transfers between devices, shards(): lax.all_gather(gate_delta, 'row', axis=0, tiled=True)  64.6 us
    all_gather x1, waiting for transfers between devices, shards(): lax.all_gather(up_delta, 'row', axis=0, tiled=True)  57.6 us
    unnamed x27, local copies, waits for them, and re-layouts  35.6 us
    mul x3, other arithmetic, masked(): pruned = blocks * block_mask[:, None, :, None].astype(weight.dtype)  32.9 us
  transfers between devices with their start and end apart: 10, of which 8 were waited for; matrix products, arithmetic and copies ran while one was open for 28% of the time, Pallas kernels for 0%

commit v1 on v0

v1 whole, which is shorter than its diff:
```python
import functools

import jax
import jax.numpy as jnp
from jax import lax
from jax.experimental import pallas as pl
from jax.experimental.pallas import tpu as pltpu
from jax.sharding import PartitionSpec as P

loss_scale = 8.0
F32 = jnp.float32
BF16 = jnp.bfloat16
MESH = pl.DeviceIdType.MESH


def classify(logits, labels):
    exponent = jnp.exp(logits)
    partition = jnp.sum(exponent, axis=1, keepdims=True)
    classes = lax.broadcasted_iota(jnp.int32, logits.shape, 1)
    onehot = (labels[:, None] == classes).astype(F32)
    token_cost = jnp.log(partition[:, 0]) - jnp.sum(logits * onehot, axis=1)
    return (token_cost, loss_scale * (exponent / partition - onehot))


def tile_of(width):
    for tile in (512, 256, 128):
        if width % tile == 0:
            return tile
    return width


def widened(mask, width):
    return jnp.repeat(mask.astype(F32), width // mask.shape[1], axis=1)


def pruned(values, mask):
    height, breadth = values.shape
    blocks = mask.shape[0]
    split = values.reshape(blocks, height // blocks, breadth)
    kept = split * mask[:, None, :].astype(values.dtype)
    return kept.reshape(height, breadth)


def dot(a, b, a_axis, b_axis):
    return lax.dot_general(a, b, (((a_axis,), (b_axis,)), ((), ())), preferred_element_type=F32)


def run(body, grid, in_specs, out_specs, out_shape, flops, touched, scratch=()):
    return pl.pallas_call(
        body,
        grid=grid,
        in_specs=in_specs,
        out_specs=out_specs,
        out_shape=out_shape,
        scratch_shapes=list(scratch),
        compiler_params=pltpu.CompilerParams(vmem_limit_bytes=40 << 20),
        cost_estimate=pl.CostEstimate(flops=flops, bytes_accessed=touched, transcendentals=0),
    )


def gate_up_parts(x, gate, up, gate_mask, up_mask, rows):
    tokens, depth = x.shape
    width = gate.shape[1]
    tile = tile_of(width)
    blocks = gate_mask.shape[0]

    def body(x_ref, g_ref, u_ref, gm_ref, um_ref, o_ref):
        for k, (w, m) in enumerate(((g_ref, gm_ref), (u_ref, um_ref))):
            part = dot(x_ref[...], pruned(w[...], m[...]), 1, 0).astype(BF16)
            o_ref[:, k] = part.reshape(rows, tokens // rows, tile)

    weight = pl.BlockSpec((depth, tile), lambda j: (0, j))
    mask = pl.BlockSpec((blocks, tile), lambda j: (0, j))
    return run(
        body,
        (width // tile,),
        [pl.BlockSpec((tokens, depth), lambda j: (0, 0)), weight, weight, mask, mask],
        pl.BlockSpec((rows, 2, tokens // rows, tile), lambda j: (0, 0, 0, j)),
        jax.ShapeDtypeStruct((rows, 2, tokens // rows, width), BF16),
        4 * tokens * depth * width,
        4 * depth * width + 4 * tokens * width,
    )(x, gate, up, gate_mask, up_mask)


def down_part(hidden, down, mask):
    tokens, width = hidden.shape
    depth = down.shape[1]
    tile = tile_of(width)
    steps = width // tile
    mask = mask.reshape(steps, -1, depth)

    def body(h_ref, w_ref, m_ref, o_ref, acc):
        j = pl.program_id(0)
        part = dot(h_ref[...], pruned(w_ref[...], m_ref[0]), 1, 0)

        @pl.when(j == 0)
        def _():
            acc[...] = part

        @pl.when(j > 0)
        def _():
            acc[...] += part

        @pl.when(j == steps - 1)
        def _():
            o_ref[...] = acc[...].astype(BF16)

    return run(
        body,
        (steps,),
        [
            pl.BlockSpec((tokens, tile), lambda j: (0, j)),
            pl.BlockSpec((tile, depth), lambda j: (j, 0)),
            pl.BlockSpec((1, mask.shape[1], depth), lambda j: (j, 0, 0)),
        ],
        pl.BlockSpec((tokens, depth), lambda j: (0, 0)),
        jax.ShapeDtypeStruct((tokens, depth), BF16),
        2 * tokens * depth * width,
        2 * depth * width + 2 * tokens * width,
        [pltpu.VMEM((tokens, depth), F32)],
    )(hidden, down, mask)


def dhidden_part(dmixed, down, mask):
    tokens, depth = dmixed.shape
    width = down.shape[0]
    tile = tile_of(width)
    steps = width // tile
    mask = mask.reshape(steps, -1, depth)

    def body(d_ref, w_ref, m_ref, o_ref):
        o_ref[...] = dot(d_ref[...], pruned(w_ref[...], m_ref[0]), 1, 1).astype(BF16)

    return run(
        body,
        (steps,),
        [
            pl.BlockSpec((tokens, depth), lambda j: (0, 0)),
            pl.BlockSpec((tile, depth), lambda j: (j, 0)),
            pl.BlockSpec((1, mask.shape[1], depth), lambda j: (j, 0, 0)),
        ],
        pl.BlockSpec((tokens, tile), lambda j: (0, j)),
        jax.ShapeDtypeStruct((tokens, width), BF16),
        2 * tokens * depth * width,
        2 * depth * width + 2 * tokens * width,
    )(dmixed, down, mask)


def input_part(gate_delta, up_delta, gate, up, gate_mask, up_mask):
    tokens, width = gate_delta.shape
    depth = gate.shape[0]
    tile = tile_of(width)
    steps = width // tile
    blocks = gate_mask.shape[0]

    def body(gd_ref, ud_ref, g_ref, u_ref, gm_ref, um_ref, o_ref, acc):
        j = pl.program_id(0)
        part = dot(gd_ref[...], pruned(g_ref[...], gm_ref[...]), 1, 1)
        part += dot(ud_ref[...], pruned(u_ref[...], um_ref[...]), 1, 1)

        @pl.when(j == 0)
        def _():
            acc[...] = part

        @pl.when(j > 0)
        def _():
            acc[...] += part

        @pl.when(j == steps - 1)
        def _():
            o_ref[...] = acc[...].astype(BF16)

    delta = pl.BlockSpec((tokens, tile), lambda j: (0, j))
    weight = pl.BlockSpec((depth, tile), lambda j: (0, j))
    mask = pl.BlockSpec((blocks, tile), lambda j: (0, j))
    return run(
        body,
        (steps,),
        [delta, delta, weight, weight, mask, mask],
        pl.BlockSpec((tokens, depth), lambda j: (0, 0)),
        jax.ShapeDtypeStruct((tokens, depth), BF16),
        4 * tokens * depth * width,
        4 * depth * width + 4 * tokens * width,
        [pltpu.VMEM((tokens, depth), F32)],
    )(gate_delta, up_delta, gate, up, gate_mask, up_mask)


def column_grad(x, delta, mask):
    tokens, depth = x.shape
    width = delta.shape[1]
    tile = tile_of(width)
    blocks = mask.shape[0]

    def body(x_ref, d_ref, m_ref, o_ref):
        o_ref[...] = pruned(dot(x_ref[...], d_ref[...], 0, 0), m_ref[...]).astype(BF16)

    return run(
        body,
        (width // tile,),
        [
            pl.BlockSpec((tokens, depth), lambda j: (0, 0)),
            pl.BlockSpec((tokens, tile), lambda j: (0, j)),
            pl.BlockSpec((blocks, tile), lambda j: (0, j)),
        ],
        pl.BlockSpec((depth, tile), lambda j: (0, j)),
        jax.ShapeDtypeStruct((depth, width), BF16),
        2 * tokens * depth * width,
        2 * depth * width + 2 * tokens * width,
    )(x, delta, mask)


def row_grad(hidden, dmixed, mask):
    tokens, width = hidden.shape
    depth = dmixed.shape[1]
    tile = tile_of(width)
    steps = width // tile
    mask = mask.reshape(steps, -1, depth)

    def body(h_ref, d_ref, m_ref, o_ref):
        o_ref[...] = pruned(dot(h_ref[...], d_ref[...], 0, 0), m_ref[0]).astype(BF16)

    return run(
        body,
        (steps,),
        [
            pl.BlockSpec((tokens, tile), lambda j: (0, j)),
            pl.BlockSpec((tokens, depth), lambda j: (0, 0)),
            pl.BlockSpec((1, mask.shape[1], depth), lambda j: (j, 0, 0)),
        ],
        pl.BlockSpec((tile, depth), lambda j: (j, 0)),
        jax.ShapeDtypeStruct((width, depth), BF16),
        2 * tokens * depth * width,
        2 * depth * width + 2 * tokens * width,
    )(hidden, dmixed, mask)


def grid_of(axis, fast, size):
    me = lax.axis_index(axis)
    return me, lax.div(me, fast), lax.rem(me, fast), size // fast


def greet(axis, slow, quick, slows, fast):
    barrier = pltpu.get_barrier_semaphore()
    for d in range(1, fast):
        there = slow * fast + lax.rem(quick + d, fast)
        pl.semaphore_signal(barrier, inc=1, device_id={axis: there}, device_id_type=MESH)
    for d in range(1, slows):
        there = lax.rem(slow + d, slows) * fast + quick
        pl.semaphore_signal(barrier, inc=1, device_id={axis: there}, device_id_type=MESH)
    pl.semaphore_wait(barrier, fast + slows - 2)


def send(src, dst, sems, where, axis, there):
    copy = pltpu.make_async_remote_copy(
        src_ref=src,
        dst_ref=dst,
        send_sem=sems[0].at[where],
        recv_sem=sems[1].at[where],
        device_id={axis: there},
        device_id_type=MESH,
    )
    copy.start()
    return copy


def talking(call_id):
    return pltpu.CompilerParams(
        collective_id=call_id, has_side_effects=True, vmem_limit_bytes=56 << 20
    )


def both(*dims):
    return [pltpu.SemaphoreType.DMA(dims), pltpu.SemaphoreType.DMA(dims)]


def reduce_scatter(parts, axis, fast, slices, call_id):
    size, height, width = parts.shape
    slows = size // fast
    step = height // slices
    group = 16

    def body(p_ref, o_ref, xbuf, ybuf, zbuf, *sems):
        xsems, zsems = sems[:2], sems[2:]
        _, slow, quick, _ = grid_of(axis, fast, size)
        greet(axis, slow, quick, slows, fast)
        order = [(d, s) for s in range(slices) for d in [*range(1, slows), 0]]
        xcopies, zcopies = {}, {}
        for d, s in order:
            a = lax.rem(slow + d, slows)
            cut = pl.ds(s * step, step)
            for e in range(1, fast):
                b = lax.rem(quick + e, fast)
                xcopies[d, s, e] = send(
                    p_ref.at[a * fast + b, cut],
                    xbuf.at[e - 1, d, cut],
                    xsems,
                    (d * slices + s) * (fast - 1) + e - 1,
                    axis,
                    slow * fast + b,
                )
        for d, s in order:
            a = lax.rem(slow + d, slows)
            for e in range(1, fast):
                xcopies[d, s, e].wait_recv()

            def add(i, carry, d=d, s=s, a=a):
                at = pl.ds(pl.multiple_of(s * step + i * group, group), group)
                total = p_ref[a * fast + quick, at].astype(F32)
                for e in range(1, fast):
                    total += xbuf[e - 1, d, at].astype(F32)
                if d == 0:
                    o_ref[at] = total
                else:
                    ybuf[d - 1, at] = total.astype(BF16)
                return carry

            lax.fori_loop(0, step // group, add, 0)
            if d:
                cut = pl.ds(s * step, step)
                zcopies[d, s] = send(
                    ybuf.at[d - 1, cut],
                    zbuf.at[d - 1, cut],
                    zsems,
                    (d - 1) * slices + s,
                    axis,
                    a * fast + quick,
                )
        for s in range(slices):
            for d in range(1, slows):
                zcopies[d, s].wait_recv()

            def close(i, carry, s=s):
                at = pl.ds(pl.multiple_of(s * step + i * group, group), group)
                total = o_ref[at]
                for d in range(1, slows):
                    total += zbuf[d - 1, at].astype(F32)
                o_ref[at] = total
                return carry

            lax.fori_loop(0, step // group, close, 0)
        for copy in [*xcopies.values(), *zcopies.values()]:
            copy.wait_send()

    return pl.pallas_call(
        body,
        in_specs=[pl.BlockSpec(memory_space=pltpu.VMEM)],
        out_specs=pl.BlockSpec(memory_space=pltpu.VMEM),
        out_shape=jax.ShapeDtypeStruct((height, width), F32),
        scratch_shapes=[
            pltpu.VMEM((fast - 1, slows, height, width), BF16),
            pltpu.VMEM((slows - 1, height, width), BF16),
            pltpu.VMEM((slows - 1, height, width), BF16),
            *both(slows * slices * (fast - 1)),
            *both((slows - 1) * slices),
        ],
        compiler_params=talking(call_id),
    )(parts)


def gather(blocks, axis, size, fast, slices, call_id):
    height, width = blocks[0].shape
    slows = size // fast
    step = height // slices
    count = len(blocks)

    def body(*refs):
        ins, outs = refs[:count], refs[count : 2 * count]
        local, *sems = refs[2 * count :]
        xsems, zsems = sems[:2], sems[2:]
        me, slow, quick, _ = grid_of(axis, fast, size)
        greet(axis, slow, quick, slows, fast)
        order = [(k, s) for k in range(count) for s in range(slices)]
        copies, zcopies = [], {}

        def across(k, s, d, src, slot):
            cut = pl.ds(s * step, step)
            for e in range(1, fast):
                b = lax.rem(quick + e, fast)
                where = ((k * slices + s) * slows + d) * (fast - 1) + e - 1
                copies.append(
                    send(src, outs[k].at[slot, cut], xsems, where, axis, slow * fast + b)
                )

        keep = []
        for k, s in order:
            cut = pl.ds(s * step, step)
            for d in range(1, slows):
                there = lax.rem(slow + d, slows) * fast + quick
                zcopies[k, s, d] = send(
                    ins[k].at[cut],
                    outs[k].at[me, cut],
                    zsems,
                    (k * slices + s) * (slows - 1) + d - 1,
                    axis,
                    there,
                )
            across(k, s, 0, ins[k].at[cut], me)
        for k in range(count):
            keep.append(pltpu.make_async_copy(ins[k], outs[k].at[me], local.at[k]))
            keep[-1].start()
        for k, s in order:
            cut = pl.ds(s * step, step)
            for d in range(1, slows):
                slot = lax.rem(slow + slows - d, slows) * fast + quick
                zcopies[k, s, d].wait_recv()
                across(k, s, d, outs[k].at[slot, cut], slot)
        for copy in copies:
            copy.wait()
        for copy in zcopies.values():
            copy.wait_send()
        for copy in keep:
            copy.wait()

    got = pl.pallas_call(
        body,
        in_specs=[pl.BlockSpec(memory_space=pltpu.VMEM)] * count,
        out_specs=[pl.BlockSpec(memory_space=pl.ANY)] * count,
        out_shape=[jax.ShapeDtypeStruct((size, height, width), BF16)] * count,
        scratch_shapes=[
            pltpu.SemaphoreType.DMA((count,)),
            *both(count * slices * slows * (fast - 1)),
            *both(count * slices * (slows - 1)),
        ],
        compiler_params=talking(call_id),
    )(*blocks)
    return [whole.reshape(size * height, width) for whole in got]


def total_over(part, axis, size, fast, call_id):
    height, width = part.shape
    slows = size // fast

    def body(p_ref, o_ref, xbuf, ysum, zbuf, *sems):
        xsems, zsems = sems[:2], sems[2:]
        _, slow, quick, _ = grid_of(axis, fast, size)
        greet(axis, slow, quick, slows, fast)
        copies = []
        for e in range(1, fast):
            b = lax.rem(quick + e, fast)
            copies.append(send(p_ref, xbuf.at[quick], xsems, e - 1, axis, slow * fast + b))
        xbuf[quick] = p_ref[...]
        for copy in copies:
            copy.wait()
        total = xbuf[0]
        for b in range(1, fast):
            total += xbuf[b]
        ysum[...] = total
        copies = []
        for d in range(1, slows):
            there = lax.rem(slow + d, slows) * fast + quick
            copies.append(send(ysum, zbuf.at[slow], zsems, d - 1, axis, there))
        zbuf[slow] = total
        for copy in copies:
            copy.wait()
        total = zbuf[0]
        for a in range(1, slows):
            total += zbuf[a]
        o_ref[...] = total

    return pl.pallas_call(
        body,
        in_specs=[pl.BlockSpec(memory_space=pltpu.VMEM)],
        out_specs=pl.BlockSpec(memory_space=pltpu.VMEM),
        out_shape=jax.ShapeDtypeStruct((height, width), F32),
        scratch_shapes=[
            pltpu.VMEM((fast, height, width), F32),
            pltpu.VMEM((height, width), F32),
            pltpu.VMEM((slows, height, width), F32),
            *both(fast - 1),
            *both(slows - 1),
        ],
        compiler_params=talking(call_id),
    )(part)


def shards(
    rows, cols, tokens, gate_weight, up_weight, down_weight, gate_mask, up_mask, down_mask, head_weight, labels
):
    width = gate_weight.shape[1]
    gate_mask = widened(gate_mask, width)
    up_mask = widened(up_mask, width)
    down_mask = widened(down_mask, down_weight.shape[1])
    near = rows // 4
    mine = tokens.shape[0]
    (every_token,) = gather([tokens], "col", cols, 2, 2, 1)
    parts = gate_up_parts(every_token, gate_weight, up_weight, gate_mask, up_mask, rows)
    share = parts.shape[2]
    stacked = reduce_scatter(parts.reshape(rows, 2 * share, width), "row", near, 4, 2)
    gate_sum, up_sum = stacked[:share], stacked[share:]
    sigmoid_gate = jax.nn.sigmoid(gate_sum)
    activated = gate_sum * sigmoid_gate
    hidden = (activated * up_sum).astype(BF16)
    (hidden_all,) = gather([hidden], "row", rows, near, 4, 3)
    branch = reduce_scatter(
        down_part(hidden_all, down_weight, down_mask).reshape(cols, mine, -1), "col", 2, 2, 4
    )
    mixed_rows = (tokens.astype(F32) + branch).astype(BF16)
    partial_value = jnp.dot(mixed_rows, head_weight, preferred_element_type=F32)
    logits = total_over(partial_value, "row", rows, near, 5)
    token_loss, grad_full = classify(logits, labels)
    dlogits = grad_full.astype(BF16)
    dmixed = dot(dlogits, head_weight, 1, 1).astype(BF16)
    (dmixed_all,) = gather([dmixed], "col", cols, 2, 2, 6)
    dhidden = reduce_scatter(
        dhidden_part(dmixed_all, down_weight, down_mask).reshape(rows, share, width), "row", near, 4, 7
    )
    gate_delta = (dhidden * up_sum * sigmoid_gate * (1.0 + gate_sum * (1.0 - sigmoid_gate))).astype(BF16)
    up_delta = (dhidden * activated).astype(BF16)
    gate_all, up_all = gather([gate_delta, up_delta], "row", rows, near, 4, 8)
    down_grad = row_grad(hidden_all, dmixed_all, down_mask)
    gate_grad = column_grad(every_token, gate_all, gate_mask)
    up_grad = column_grad(every_token, up_all, up_mask)
    input_sum = lax.psum_scatter(
        input_part(gate_all, up_all, gate_weight, up_weight, gate_mask, up_mask),
        "col",
        scatter_dimension=0,
        tiled=True,
    ).astype(F32)
    tokens_grad = (dmixed.astype(F32) + input_sum).astype(BF16)
    return (token_loss, tokens_grad, gate_grad, up_grad, down_grad)


def solution(mesh):
    placed = (
        P("col", "row"),
        P("row", "col"),
        P("row", "col"),
        P("col", "row"),
        P("row", "col"),
        P("row", "col"),
        P("col", "row"),
        P("row", None),
        P("col"),
    )
    return jax.shard_map(
        functools.partial(shards, mesh.shape["row"], mesh.shape["col"]),
        mesh=mesh,
        in_specs=placed,
        out_specs=(P("col"), P("col", "row"), P("row", "col"), P("row", "col"), P("col", "row")),
        check_vma=False,
    )
```

time: 1020 us -> 460 us (0.45)
  waiting for transfers between devices: 640 us -> 4.02 us
  Pallas kernels: 0 us -> 403 us
  local copies, waits for them, and re-layouts: 226 us -> 23.7 us
  matrix products: 83.3 us -> 3.72 us
  other arithmetic: 47.7 us -> 10.4 us
    pallas_call x0 -> x15, Pallas kernels: none -> 403 us  [the longest x4 170 us: gather(): pl.pallas_call(body, in_specs=[pl.BlockSpec(memory_space=pltpu.VMEM)] * c...]
    reduce_scatter x4 -> x1, waiting for transfers between devices: 403 us -> 4.01 us  [shards(): lax.psum_scatter(input_part(gate_all, up_all, gate_weight, up_weight, gat...]
    mul x12 -> x0, local copies, waits for them, and re-layouts: 190 us -> none  [masked(): pruned = blocks * block_mask[:, None, :, None].astype(weight.dtype)]
    all_gather x5 -> x0, waiting for transfers between devices: 164 us -> none  [the longest x1 64.6 us: shards(): lax.all_gather(gate_delta, 'row', axis=0, tiled=True)]
    psum x1 -> x0, waiting for transfers between devices: 71.2 us -> none  [shards(): logits = lax.psum(partial_value, 'row')]
    dot_general x10 -> x2, matrix products: 73 us -> 3.72 us  [the longest x1 1.9 us: shards(): partial_value = jnp.dot(mixed_rows, head_weight, preferred_element_type=F32)]
    mul x3 -> x0, other arithmetic: 32.9 us -> none  [masked(): pruned = blocks * block_mask[:, None, :, None].astype(weight.dtype)]
    unnamed x27 -> x42, local copies, waits for them, and re-layouts: 35.6 us -> 22.6 us
  transfers between devices with their start and end apart: 10 -> 1, of which waited for: 8 -> 1; matrix products, arithmetic and copies ran while one was open for 28% -> 0% of each run, Pallas kernels for 0% -> 5%
where the time goes in v1:
time: 460 us; the launch traced here: 459 us
  Pallas kernels  403 us (88%)
  local copies, waits for them, and re-layouts  23.7 us (5%)
  between operations  14.3 us (3%)
  other arithmetic  10.4 us (2%)
    pallas_call x4, Pallas kernels, gather(): pl.pallas_call(body, in_specs=[pl.BlockSpec(memory_space=pltpu.VMEM)] * c...  170 us
    pallas_call x3, Pallas kernels, reduce_scatter(): pl.pallas_call(body, in_specs=[pl.BlockSpec(memory_space=pltpu.VMEM)], ou...  159 us
    unnamed x42, local copies, waits for them, and re-layouts  22.6 us
    pallas_call x1, Pallas kernels, total_over(): pl.pallas_call(body, in_specs=[pl.BlockSpec(memory_space=pltpu.VMEM)], ou...  15.8 us
    pallas_call x2, Pallas kernels, column_grad(): run(body, (width // tile,), [pl.BlockSpec((tokens, depth), lambda j: (0,...  14.1 us
    pallas_call x1, Pallas kernels, input_part(): run(body, (steps,), [delta, delta, weight, weight, mask, mask], pl.BlockS...  13.7 us
    pallas_call x1, Pallas kernels, gate_up_parts(): run(body, (width // tile,), [pl.BlockSpec((tokens, depth), lambda j: (0,...  11.6 us
  transfers between devices with their start and end apart: 1, of which 1 were waited for; matrix products, arithmetic and copies ran while one was open for 0% of the time, Pallas kernels for 5%

profile of v1, /device:TPU:0, one launch (start us, length us, event | category | flops | bytes accessed | tf_op | source)
XLA Modules:
  0.0 459.0 jit_solution(12583186560004035753)
XLA Ops:
  10.4 12.5 %shard_map.128 = bf16[4,128,1024]{2,1,0:T(8,128)(2,1)} custom-call(bf16[128,1024]{1,0:T(8,128)(2,1)} %refs_0_.1), custom_call_target="tpu_custom_call" | custom-call | tf_op jit(solution)/shard_map/pallas_call | solution.py:414
  22.9 1.2 copy-done.6
  24.2 11.6 %shard_map.129 = bf16[8,2,64,3584]{3,2,1,0:T(8,128)(2,1)S(1)} custom-call(bf16[512,1024]{1,0:T(8,128)(2,1)S(1)} %bitcast.14, bf16[1024,3584]{1,0:T(8,128)(2,1)} %g_ref.3, bf16[1024,3584]{1,0:T(8,128)(2,1)} %u_ref.3, f32[16,3584]{1,0:T(8,128)S(1)} %reshape.43.gm_ref.m_ref, f32[16,3584]{1,0:T(8,128)S(1)} %reshape.44.um_ref.m_ref), custom_call_target="tpu_custom_call" | custom-call | flops 7516192768 | bytes 22020096 | tf_op jit(solution)/shard_map/pallas_call | solution.py:74
  35.7 3.0 copy-done.2
  38.8 95.5 %shard_map.130 = f32[128,3584]{1,0:T(8,128)} custom-call(bf16[8,128,3584]{2,1,0:T(8,128)(2,1)} %bitcast.10), custom_call_target="tpu_custom_call" | custom-call | tf_op jit(solution)/shard_map/pallas_call | solution.py:344
  134.3 2.5 multiply_convert_fusion.2.refs_0_
  136.8 50.7 %shard_map.131 = bf16[8,64,3584]{2,1,0:T(8,128)(2,1)} custom-call(bf16[64,3584]{1,0:T(8,128)(2,1)} %multiply_convert_fusion.2.refs_0_), custom_call_target="tpu_custom_call" | custom-call | tf_op jit(solution)/shard_map/pallas_call | solution.py:414
  187.5 2.0 copy-done.3
  189.6 3.1 copy-done.11
  192.7 6.8 %shard_map.132 = bf16[512,1024]{1,0:T(8,128)(2,1)S(1)} custom-call(bf16[512,3584]{1,0:T(8,128)(2,1)S(1)} %bitcast.11, bf16[3584,1024]{1,0:T(8,128)(2,1)S(1)} %copy-done.11, f32[7,8,1024]{2,1,0:T(8,128)S(1)} %reshape_reshape.2.m_ref), custom_call_target="tpu_custom_call" | custom-call | flops 3758096384 | bytes 11010048 | tf_op jit(solution)/shard_map/pallas_call | solution.py:108
  200.4 11.5 %shard_map.133 = f32[128,1024]{1,0:T(8,128)} custom-call(bf16[4,128,1024]{2,1,0:T(8,128)(2,1)} %bitcast.19), custom_call_target="tpu_custom_call" | custom-call | tf_op jit(solution)/shard_map/pallas_call | solution.py:344
  212.0 1.9 fusion.1.p_ref
  213.9 15.8 %shard_map.134 = f32[128,128]{1,0:T(8,128)} custom-call(f32[128,128]{1,0:T(8,128)} %fusion.1.p_ref), custom_call_target="tpu_custom_call" | custom-call | tf_op jit(solution)/shard_map/pallas_call | solution.py:460
  229.7 1.0 exponential_reduce_fusion
  230.7 1.8 convolution_convert_fusion.refs_0_
  232.6 10.3 %shard_map.135 = bf16[4,128,1024]{2,1,0:T(8,128)(2,1)} custom-call(bf16[128,1024]{1,0:T(8,128)(2,1)} %convolution_convert_fusion.refs_0_), custom_call_target="tpu_custom_call" | custom-call | tf_op jit(solution)/shard_map/pallas_call | solution.py:414
  242.9 1.2 copy-done.8
  244.1 3.1 copy-done.12
  247.2 5.5 %shard_map.136 = bf16[512,3584]{1,0:T(8,128)(2,1)S(1)} custom-call(bf16[512,1024]{1,0:T(8,128)(2,1)S(1)} %bitcast.17, bf16[3584,1024]{1,0:T(8,128)(2,1)S(1)} %copy-done.12, f32[7,8,1024]{2,1,0:T(8,128)S(1)} %reshape_reshape.2.m_ref), custom_call_target="tpu_custom_call" | custom-call | flops 3758096384 | bytes 11010048 | tf_op jit(solution)/shard_map/pallas_call | solution.py:134
  252.7 1.8 copy-done.5
  254.6 51.5 %shard_map.137 = f32[64,3584]{1,0:T(8,128)} custom-call(bf16[8,64,3584]{2,1,0:T(8,128)(2,1)} %bitcast.13), custom_call_target="tpu_custom_call" | custom-call | tf_op jit(solution)/shard_map/pallas_call | solution.py:344
  306.0 2.5 multiply_convert_fusion
  308.6 96.4 %shard_map.138 = (bf16[8,64,3584]{2,1,0:T(8,128)(2,1)}, bf16[8,64,3584]{2,1,0:T(8,128)(2,1)}) custom-call(bf16[64,3584]{1,0:T(8,128)(2,1)} %get-tuple-element.12.refs_0_, bf16[64,3584]{1,0:T(8,128)(2,1)} %get-tuple-element.11.refs_1_), custom_call_target="tpu_custom_call" | custom-call | tf_op jit(solution)/shard_map/pallas_call | solution.py:414
  405.0 2.0 copy-done.13
  407.0 2.0 copy-done.15
  409.0 13.7 %shard_map.139 = bf16[512,1024]{1,0:T(8,128)(2,1)} custom-call(bf16[512,3584]{1,0:T(8,128)(2,1)S(1)} %bitcast.20, bf16[512,3584]{1,0:T(8,128)(2,1)S(1)} %bitcast.22, bf16[1024,3584]{1,0:T(8,128)(2,1)} %g_ref.3, bf16[1024,3584]{1,0:T(8,128)(2,1)} %u_ref.3, f32[16,3584]{1,0:T(8,128)S(1)} %reshape.43.gm_ref.m_ref, f32[16,3584]{1,0:T(8,128)S(1)} %reshape.44.um_ref.m_ref), custom_call_target="tpu_custom_call" | custom-call | flops 7516192768 | bytes 22020096 | tf_op jit(solution)/shard_map/pallas_call | solution.py:176
  423.3 2.0 copy-done.4
  425.4 7.0 %shard_map.142 = bf16[3584,1024]{1,0:T(8,128)(2,1)} custom-call(bf16[512,3584]{1,0:T(8,128)(2,1)S(1)} %bitcast.12, bf16[512,1024]{1,0:T(8,128)(2,1)S(1)} %bitcast.18, f32[7,8,1024]{2,1,0:T(8,128)S(1)} %reshape_reshape.2.m_ref), custom_call_target="tpu_custom_call" | custom-call | flops 3758096384 | bytes 11010048 | tf_op jit(solution)/shard_map/pallas_call | solution.py:222
  432.4 7.0 %shard_map.141 = bf16[1024,3584]{1,0:T(8,128)(2,1)} custom-call(bf16[512,1024]{1,0:T(8,128)(2,1)S(1)} %bitcast.15, bf16[512,3584]{1,0:T(8,128)(2,1)S(1)} %bitcast.23, f32[16,3584]{1,0:T(8,128)S(1)} %reshape.44.um_ref.m_ref), custom_call_target="tpu_custom_call" | custom-call | flops 3758096384 | bytes 11010048 | tf_op jit(solution)/shard_map/pallas_call | solution.py:197
  439.4 7.0 %shard_map.140 = bf16[1024,3584]{1,0:T(8,128)(2,1)} custom-call(bf16[512,1024]{1,0:T(8,128)(2,1)S(1)} %bitcast.16, bf16[512,3584]{1,0:T(8,128)(2,1)S(1)} %bitcast.21, f32[16,3584]{1,0:T(8,128)S(1)} %reshape.43.gm_ref.m_ref), custom_call_target="tpu_custom_call" | custom-call | flops 3758096384 | bytes 11010048 | tf_op jit(solution)/shard_map/pallas_call | solution.py:197
  446.5 4.0 reduce-scatter.2.cloned.1.call-done
  450.5 1.7 add_convert_fusion
  (45 shorter events, 4.8 us)
Async XLA Ops:
  7.2 204.8 %copy-start = (bf16[1024,128]{1,0:T(8,128)(2,1)S(1)}, bf16[1024,128]{1,0:T(8,128)(2,1)}, u32[]{:S(2)}) copy-start(bf16[1024,128]{1,0:T(8,128)(2,1)} %param.16) | copy-start | bytes 786436
  7.2 443.3 %reduce-scatter.2.cloned.1.call-start = ((), (), s32[]{:S(2)}) async-start(), calls=%async_computation.1 | async-start | bytes 1310720 | tf_op jit(solution)/shard_map/reduce_scatter | solution.py:513
  22.9 1.2 copy-start.6
  35.7 3.1 copy-start.2
  187.5 2.0 copy-start.3
  189.6 3.1 copy-start.11
  192.6 19.3 %copy-start.19 = (bf16[128,1024]{1,0:T(8,128)(2,1)S(1)}, bf16[128,1024]{1,0:T(8,128)(2,1)}, u32[]{:S(2)}) copy-start(bf16[128,1024]{1,0:T(8,128)(2,1)} %refs_0_.1) | copy-start | bytes 786436
  192.7 37.1 %copy-start.20 = (s32[128]{0:T(128)S(1)}, s32[128]{0:T(128)}, u32[]{:S(2)}) copy-start(s32[128]{0:T(128)} %param.17) | copy-start | bytes 1540
  199.5 1.0 copy-start.10
  242.9 1.2 copy-start.8
  244.1 3.1 copy-start.12
  247.2 58.8 %copy-start.17 = (f32[128,3584]{1,0:T(8,128)S(1)}, f32[128,3584]{1,0:T(8,128)}, u32[]{:S(2)}) copy-start(f32[128,3584]{1,0:T(8,128)} %shard_map.130) | copy-start | bytes 5505028
  252.7 1.8 copy-start.5
  404.9 2.0 copy-start.13
  407.0 2.0 copy-start.15
  409.0 14.3 %copy-start.9 = (bf16[4,128,1024]{2,1,0:T(8,128)(2,1)S(1)}, bf16[4,128,1024]{2,1,0:T(8,128)(2,1)}, u32[]{:S(2)}) copy-start(bf16[4,128,1024]{2,1,0:T(8,128)(2,1)} %shard_map.135) | copy-start | bytes 3145732
  422.8 9.6 %copy-start.7 = (bf16[4,128,1024]{2,1,0:T(8,128)(2,1)S(1)}, bf16[4,128,1024]{2,1,0:T(8,128)(2,1)}, u32[]{:S(2)}) copy-start(bf16[4,128,1024]{2,1,0:T(8,128)(2,1)} %shard_map.128) | copy-start | bytes 3145732
  423.3 2.0 copy-start.4
  425.4 7.0 %copy-start.16 = (bf16[8,64,3584]{2,1,0:T(8,128)(2,1)S(1)}, bf16[8,64,3584]{2,1,0:T(8,128)(2,1)}, u32[]{:S(2)}) copy-start(bf16[8,64,3584]{2,1,0:T(8,128)(2,1)} %get-tuple-element.8) | copy-start | bytes 11010052
  432.4 7.1 %copy-start.14 = (bf16[8,64,3584]{2,1,0:T(8,128)(2,1)S(1)}, bf16[8,64,3584]{2,1,0:T(8,128)(2,1)}, u32[]{:S(2)}) copy-start(bf16[8,64,3584]{2,1,0:T(8,128)(2,1)} %get-tuple-element.7) | copy-start | bytes 11010052
  432.4 19.8 %copy-start.1 = (bf16[1024,128]{1,0:T(8,128)(2,1)S(1)}, bf16[1024,128]{1,0:T(8,128)(2,1)}, u32[]{:S(2)}) copy-start(bf16[1024,128]{1,0:T(8,128)(2,1)} %param.16) | copy-start | bytes 786436
  439.4 11.0 %copy-start.18 = (bf16[128,1024]{1,0:T(8,128)(2,1)S(1)}, bf16[128,1024]{1,0:T(8,128)(2,1)}, u32[]{:S(2)}) copy-start(bf16[128,1024]{1,0:T(8,128)(2,1)} %convolution_convert_fusion.refs_0_) | copy-start | bytes 786436
Sparse Core Ops, SparseCore 0:
  422.9 27.4 reduce-scatter.1
